TPU v7x, 32 devices: a whole 2x2x4 slice. The times are simulated.
32 devices in a mesh: section: 4 (over z), tm: 8 (over y, x, core).
Axes of the slice: x: 2, y: 2, z: 4, core: 2. Of those that a mesh axis runs over, the one named last changes fastest.
Arguments:
- clean: float32 [4, 4, 512], P(None, None, 'tm'), may hold values from -6 to 6
- noise: float32 [4, 4, 512], P(None, None, 'tm'), may hold values from -6 to 6
- timestep: int32 [4], replicated, may hold values from 0 to 999
- lift: float32 [256], replicated, may hold values from -4 to 4
- norm_gain: float32 [4, 2, 256], P('section'), may hold values from 0.5 to 1.5
- norm_bias: float32 [4, 2, 256], P('section'), may hold values from -0.7 to 0.7
- conv_weight: bfloat16 [4, 2, 3, 3, 256, 256], P('section'), may hold values from -0.125 to 0.125
- time_proj: bfloat16 [4, 256, 256], P('section'), may hold values from -0.375 to 0.375
Outputs:
- skips: bfloat16 [4, 4, 4, 512, 256], P('section', None, None, 'tm')
All inputs are finite; a program needn't handle non-finite values.
Results may differ from a plain program's by a relative error of at most 0.012.
Values may be sent and summed in bfloat16 or wider, within the bound.
A program may use at most 64 MiB of HBM per device.

v0:
```python
import math

import jax
import jax.numpy as jnp
from jax import lax
from jax.sharding import PartitionSpec as P

C = 256
GROUPS = 32
LAYERS = 2
STEPS = 1000


def extended(cells, sides, width):
    for axis, dim in sides:
        count = lax.axis_size(axis)
        ends = count - 1
        head = lax.slice_in_dim(cells, 0, width, axis=dim)
        tail = lax.slice_in_dim(cells, cells.shape[dim] - width, cells.shape[dim], axis=dim)
        cells = jnp.concatenate(
            [
                lax.ppermute(tail, axis, [(i, (i + 1) % count) for i in range(ends)]),
                cells,
                lax.ppermute(head, axis, [((i + 1) % count, i) for i in range(ends)]),
            ],
            axis=dim,
        )
    return cells


def shifted(block, axis, distance):
    devices = range(lax.axis_size(axis))
    route = [(i - distance, i) for i in devices if i - distance in devices]
    return lax.ppermute(block, axis, route)


def prepare(clean, noise, timestep, lift):
    steps_f = timestep.astype(jnp.float32)
    level = jnp.cos(math.pi / 2.0 * (steps_f / STEPS + 0.008) / 1.008) ** 2
    noisy = jnp.sqrt(level)[:, None, None] * clean + jnp.sqrt(1.0 - level)[:, None, None] * noise
    lifted = (noisy[..., None] * lift).astype(jnp.bfloat16)
    half = C // 2
    freqs = jnp.exp(-math.log(10000.0) * jnp.arange(half, dtype=jnp.float32) / half)
    angles = steps_f[:, None] * freqs[None, :]
    emb = jnp.concatenate([jnp.sin(angles), jnp.cos(angles)], axis=1).astype(jnp.bfloat16)
    return (lifted, emb)


def group_act(middle, whole, gain, bias, count):
    rows_f, rows_t, width = middle.shape
    grouped = middle.reshape(rows_f, rows_t, GROUPS, width // GROUPS)
    total = jnp.sum(grouped, axis=(0, 1, 3))
    square = jnp.sum(grouped * grouped, axis=(0, 1, 3))
    total, square = lax.psum((total, square), "tm")
    mean = total / count
    var = square / count - mean * mean
    inv = lax.rsqrt(var + 1e-05)
    full = whole.reshape(whole.shape[0], whole.shape[1], GROUPS, width // GROUPS)
    normed = ((full - mean[:, None]) * inv[:, None]).reshape(whole.shape) * gain + bias
    return jax.nn.silu(normed).astype(jnp.bfloat16)


def conv_same(padded, weight):
    rows_f = padded.shape[0]
    width_out = padded.shape[1] - 2
    chans = padded.shape[2]
    framed = jnp.pad(padded, ((1, 1), (0, 0), (0, 0)))
    total = jnp.zeros((rows_f * width_out, weight.shape[3]), jnp.float32)
    for i in range(3):
        for j in range(3):
            window = framed[i : i + rows_f, j : j + width_out].reshape(-1, chans)
            total = total + jnp.dot(window, weight[i, j], preferred_element_type=jnp.float32)
    return total.reshape(rows_f, width_out, weight.shape[3])


def run_section(section_in, temb_row, gains, biases, weights, depth, start_pos, total_len, count):
    frames = section_in.shape[1]
    wide = extended(section_in, (("tm", 1),), LAYERS)
    hidden = wide.astype(jnp.float32) + temb_row
    places = start_pos - LAYERS + jnp.arange(frames + 2 * LAYERS)
    inside = ((places >= 0) & (places < total_len))[None, :, None]

    def layer_deep(layer, hidden):
        gain = lax.dynamic_index_in_dim(gains, layer, 0, keepdims=False)
        bias = lax.dynamic_index_in_dim(biases, layer, 0, keepdims=False)
        kernel = lax.dynamic_index_in_dim(weights, layer, 0, keepdims=False)
        act = group_act(hidden[:, LAYERS : LAYERS + frames], hidden, gain, bias, count)
        act = jnp.where(inside, act, jnp.zeros_like(act))
        padded = jnp.pad(act, ((0, 0), (1, 1), (0, 0)))
        updated = hidden + conv_same(padded, kernel)
        return jnp.where(layer < depth, updated, hidden)

    hidden = lax.fori_loop(0, LAYERS, layer_deep, hidden)
    return hidden[:, LAYERS : LAYERS + frames].astype(jnp.bfloat16)


def on_device(clean, noise, timestep, lift, norm_gain, norm_bias, conv_weight, time_proj):
    lifted, emb = prepare(clean, noise, timestep, lift)
    n_time = lax.axis_size("tm")
    frames = clean.shape[2]
    total_len = frames * n_time
    count = clean.shape[1] * total_len * (lifted.shape[3] // GROUPS)
    temb = jnp.dot(emb, time_proj[0], preferred_element_type=jnp.float32)
    section_id = lax.axis_index("section")
    n_section = lax.axis_size("section")
    micro_count = clean.shape[0]
    depth = jnp.where(section_id < n_section // 2, LAYERS, 1).astype(jnp.int32)
    start_pos = lax.axis_index("tm") * frames
    gains = norm_gain[0]
    biases = norm_bias[0]
    weights = conv_weight[0]

    def tick(step, carry):
        inbox, saved = carry
        micro = step - section_id
        live = (micro >= 0) & (micro < micro_count)
        picked = jnp.clip(micro, 0, micro_count - 1)
        first = lax.dynamic_index_in_dim(lifted, picked, 0, keepdims=False)
        section_in = jnp.where(section_id == 0, first, inbox)
        temb_row = lax.dynamic_index_in_dim(temb, picked, 0, keepdims=False)
        result = run_section(
            section_in, temb_row, gains, biases, weights, depth, start_pos, total_len, count
        )
        older = lax.dynamic_index_in_dim(saved, picked, 0, keepdims=False)
        saved = lax.dynamic_update_index_in_dim(saved, jnp.where(live, result, older), picked, 0)
        inbox = shifted(result, "section", 1)
        return (inbox, saved)

    inbox = jnp.zeros(lifted.shape[1:], jnp.bfloat16)
    saved = jnp.zeros(lifted.shape, jnp.bfloat16)
    inbox, saved = lax.fori_loop(0, micro_count + n_section - 1, tick, (inbox, saved))
    return saved[None]


def solution(mesh):
    in_specs = (
        P(None, None, "tm"),
        P(None, None, "tm"),
        P(),
        P(),
        P("section", None, None),
        P("section", None, None),
        P("section", None, None, None, None, None),
        P("section", None, None),
    )
    out_specs = P("section", None, None, "tm", None)
    return jax.shard_map(
        on_device, mesh=mesh, in_specs=in_specs, out_specs=out_specs, check_vma=False
    )
```

profile of v0, /device:TPU:26, one launch (start us, length us, event | category | flops | bytes accessed | tf_op | source)
XLA Modules:
  0.0 353.9 jit_solution(17370520694369814405)
XLA Ops:
  1.6 1.7 multiply_convert_fusion.1
  5.1 348.8 %while.52 = (s32[]{:T(128)}, bf16[4,64,256]{2,1,0:T(8,128)(2,1)S(1)}, bf16[4,4,64,256]{3,2,1,0:T(8,128)(2,1)}, pred[]{:T(512)}, s32[]{:T(128)}, /*index=5*/bf16[...) while((s32[]{:T(128)}, ...), condition=%wide.region_9.10_spmd, body=%wide.region_0.9_spmd.sunk | while | flops 323072448 | bytes 17984740 | solution.py:131
  6.0 1.9 collective-permute-start
  8.0 2.4 collective-permute-start.1
  11.3 1.6 collective-permute-done.1
  12.9 32.9 %while.53 = (s32[]{:T(128)}, f32[4,68,256]{2,1,0:T(8,128)S(1)}, s32[]{:T(128)}, f32[2,256]{1,0:T(2,128)S(1)}, f32[2,256]{1,0:T(2,128)S(1)}, /*index=5*/bf16[2,3,...) while((s32[]{:T(128)}, f32[4,68,256]{2,1,0:T(8,128)S(1)}, s32[]{:T(128)}, ...), condition=%wide.region_8.8_spmd.clone, body=%wide.region_1.7_spmd.clone.sunk | while | flops 322453952 | bytes 15810317 | solution.py:93
  13.4 11.4 %all-reduce.4 = (f32[32]{0:T(128)S(1)}, f32[32]{0:T(128)S(1)}) all-reduce(f32[32]{0:T(128)S(1)} %reduce_sum.59, f32[32]{0:T(128)S(1)} %reduce_sum.61), channel_id=1, replica_groups=mesh['section'=4,'tm'=8] {'tm'}, use_global_device_ids=true, to_apply=%region_7.6 | all-reduce | flops 64 | bytes 512 | tf_op jit(solution)/shard_map/while/body/eval_jaxpr/while/body/eval_jaxpr/psum | solution.py:54
  29.7 11.8 %all-reduce.4 = (f32[32]{0:T(128)S(1)}, f32[32]{0:T(128)S(1)}) all-reduce(f32[32]{0:T(128)S(1)} %reduce_sum.59, f32[32]{0:T(128)S(1)} %reduce_sum.61), channel_id=1, replica_groups=mesh['section'=4,'tm'=8] {'tm'}, use_global_device_ids=true, to_apply=%region_7.6 | all-reduce | flops 64 | bytes 512 | tf_op jit(solution)/shard_map/while/body/eval_jaxpr/while/body/eval_jaxpr/psum | solution.py:54
  47.8 6.6 %collective-permute-done.2 = bf16[4,64,256]{2,1,0:T(8,128)(2,1)S(1)} collective-permute-done((bf16[4,64,256]{2,1,0:T(8,128)(2,1)S(1)}, bf16[4,64,256]{2,1,0:T(8,128)(2,1)S(1)}, u32[]{:S(2)}, u32[]{:S(2)}) %collective-permute-start.2) | collective-permute-done | bytes 131104 | tf_op jit(solution)/shard_map/while/body/eval_jaxpr/ppermute | solution.py:34
  55.4 1.9 collective-permute-start
  57.3 2.4 collective-permute-start.1
  60.7 1.6 collective-permute-done.1
  62.3 33.5 %while.53 = (s32[]{:T(128)}, f32[4,68,256]{2,1,0:T(8,128)S(1)}, s32[]{:T(128)}, f32[2,256]{1,0:T(2,128)S(1)}, f32[2,256]{1,0:T(2,128)S(1)}, /*index=5*/bf16[2,3,...) while((s32[]{:T(128)}, f32[4,68,256]{2,1,0:T(8,128)S(1)}, s32[]{:T(128)}, ...), condition=%wide.region_8.8_spmd.clone, body=%wide.region_1.7_spmd.clone.sunk | while | flops 322453952 | bytes 15810317 | solution.py:93
  62.8 12.0 %all-reduce.4 = (f32[32]{0:T(128)S(1)}, f32[32]{0:T(128)S(1)}) all-reduce(f32[32]{0:T(128)S(1)} %reduce_sum.59, f32[32]{0:T(128)S(1)} %reduce_sum.61), channel_id=1, replica_groups=mesh['section'=4,'tm'=8] {'tm'}, use_global_device_ids=true, to_apply=%region_7.6 | all-reduce | flops 64 | bytes 512 | tf_op jit(solution)/shard_map/while/body/eval_jaxpr/while/body/eval_jaxpr/psum | solution.py:54
  79.6 11.8 %all-reduce.4 = (f32[32]{0:T(128)S(1)}, f32[32]{0:T(128)S(1)}) all-reduce(f32[32]{0:T(128)S(1)} %reduce_sum.59, f32[32]{0:T(128)S(1)} %reduce_sum.61), channel_id=1, replica_groups=mesh['section'=4,'tm'=8] {'tm'}, use_global_device_ids=true, to_apply=%region_7.6 | all-reduce | flops 64 | bytes 512 | tf_op jit(solution)/shard_map/while/body/eval_jaxpr/while/body/eval_jaxpr/psum | solution.py:54
  97.8 6.6 %collective-permute-done.2 = bf16[4,64,256]{2,1,0:T(8,128)(2,1)S(1)} collective-permute-done((bf16[4,64,256]{2,1,0:T(8,128)(2,1)S(1)}, bf16[4,64,256]{2,1,0:T(8,128)(2,1)S(1)}, u32[]{:S(2)}, u32[]{:S(2)}) %collective-permute-start.2) | collective-permute-done | bytes 131104 | tf_op jit(solution)/shard_map/while/body/eval_jaxpr/ppermute | solution.py:34
  105.3 1.9 collective-permute-start
  107.2 2.4 collective-permute-start.1
  110.6 1.6 collective-permute-done.1
  112.2 33.5 %while.53 = (s32[]{:T(128)}, f32[4,68,256]{2,1,0:T(8,128)S(1)}, s32[]{:T(128)}, f32[2,256]{1,0:T(2,128)S(1)}, f32[2,256]{1,0:T(2,128)S(1)}, /*index=5*/bf16[2,3,...) while((s32[]{:T(128)}, f32[4,68,256]{2,1,0:T(8,128)S(1)}, s32[]{:T(128)}, ...), condition=%wide.region_8.8_spmd.clone, body=%wide.region_1.7_spmd.clone.sunk | while | flops 322453952 | bytes 15810317 | solution.py:93
  112.7 12.0 %all-reduce.4 = (f32[32]{0:T(128)S(1)}, f32[32]{0:T(128)S(1)}) all-reduce(f32[32]{0:T(128)S(1)} %reduce_sum.59, f32[32]{0:T(128)S(1)} %reduce_sum.61), channel_id=1, replica_groups=mesh['section'=4,'tm'=8] {'tm'}, use_global_device_ids=true, to_apply=%region_7.6 | all-reduce | flops 64 | bytes 512 | tf_op jit(solution)/shard_map/while/body/eval_jaxpr/while/body/eval_jaxpr/psum | solution.py:54
  129.5 11.8 %all-reduce.4 = (f32[32]{0:T(128)S(1)}, f32[32]{0:T(128)S(1)}) all-reduce(f32[32]{0:T(128)S(1)} %reduce_sum.59, f32[32]{0:T(128)S(1)} %reduce_sum.61), channel_id=1, replica_groups=mesh['section'=4,'tm'=8] {'tm'}, use_global_device_ids=true, to_apply=%region_7.6 | all-reduce | flops 64 | bytes 512 | tf_op jit(solution)/shard_map/while/body/eval_jaxpr/while/body/eval_jaxpr/psum | solution.py:54
  147.7 6.6 %collective-permute-done.2 = bf16[4,64,256]{2,1,0:T(8,128)(2,1)S(1)} collective-permute-done((bf16[4,64,256]{2,1,0:T(8,128)(2,1)S(1)}, bf16[4,64,256]{2,1,0:T(8,128)(2,1)S(1)}, u32[]{:S(2)}, u32[]{:S(2)}) %collective-permute-start.2) | collective-permute-done | bytes 131104 | tf_op jit(solution)/shard_map/while/body/eval_jaxpr/ppermute | solution.py:34
  155.2 1.9 collective-permute-start
  157.1 2.4 collective-permute-start.1
  160.5 1.6 collective-permute-done.1
  162.1 33.5 %while.53 = (s32[]{:T(128)}, f32[4,68,256]{2,1,0:T(8,128)S(1)}, s32[]{:T(128)}, f32[2,256]{1,0:T(2,128)S(1)}, f32[2,256]{1,0:T(2,128)S(1)}, /*index=5*/bf16[2,3,...) while((s32[]{:T(128)}, f32[4,68,256]{2,1,0:T(8,128)S(1)}, s32[]{:T(128)}, ...), condition=%wide.region_8.8_spmd.clone, body=%wide.region_1.7_spmd.clone.sunk | while | flops 322453952 | bytes 15810317 | solution.py:93
  162.6 12.0 %all-reduce.4 = (f32[32]{0:T(128)S(1)}, f32[32]{0:T(128)S(1)}) all-reduce(f32[32]{0:T(128)S(1)} %reduce_sum.59, f32[32]{0:T(128)S(1)} %reduce_sum.61), channel_id=1, replica_groups=mesh['section'=4,'tm'=8] {'tm'}, use_global_device_ids=true, to_apply=%region_7.6 | all-reduce | flops 64 | bytes 512 | tf_op jit(solution)/shard_map/while/body/eval_jaxpr/while/body/eval_jaxpr/psum | solution.py:54
  179.4 11.8 %all-reduce.4 = (f32[32]{0:T(128)S(1)}, f32[32]{0:T(128)S(1)}) all-reduce(f32[32]{0:T(128)S(1)} %reduce_sum.59, f32[32]{0:T(128)S(1)} %reduce_sum.61), channel_id=1, replica_groups=mesh['section'=4,'tm'=8] {'tm'}, use_global_device_ids=true, to_apply=%region_7.6 | all-reduce | flops 64 | bytes 512 | tf_op jit(solution)/shard_map/while/body/eval_jaxpr/while/body/eval_jaxpr/psum | solution.py:54
  197.6 6.6 %collective-permute-done.2 = bf16[4,64,256]{2,1,0:T(8,128)(2,1)S(1)} collective-permute-done((bf16[4,64,256]{2,1,0:T(8,128)(2,1)S(1)}, bf16[4,64,256]{2,1,0:T(8,128)(2,1)S(1)}, u32[]{:S(2)}, u32[]{:S(2)}) %collective-permute-start.2) | collective-permute-done | bytes 131104 | tf_op jit(solution)/shard_map/while/body/eval_jaxpr/ppermute | solution.py:34
  205.1 1.9 collective-permute-start
  207.0 2.4 collective-permute-start.1
  212.0 33.5 %while.53 = (s32[]{:T(128)}, f32[4,68,256]{2,1,0:T(8,128)S(1)}, s32[]{:T(128)}, f32[2,256]{1,0:T(2,128)S(1)}, f32[2,256]{1,0:T(2,128)S(1)}, /*index=5*/bf16[2,3,...) while((s32[]{:T(128)}, f32[4,68,256]{2,1,0:T(8,128)S(1)}, s32[]{:T(128)}, ...), condition=%wide.region_8.8_spmd.clone, body=%wide.region_1.7_spmd.clone.sunk | while | flops 322453952 | bytes 15810317 | solution.py:93
  212.5 12.0 %all-reduce.4 = (f32[32]{0:T(128)S(1)}, f32[32]{0:T(128)S(1)}) all-reduce(f32[32]{0:T(128)S(1)} %reduce_sum.59, f32[32]{0:T(128)S(1)} %reduce_sum.61), channel_id=1, replica_groups=mesh['section'=4,'tm'=8] {'tm'}, use_global_device_ids=true, to_apply=%region_7.6 | all-reduce | flops 64 | bytes 512 | tf_op jit(solution)/shard_map/while/body/eval_jaxpr/while/body/eval_jaxpr/psum | solution.py:54
  229.3 11.8 %all-reduce.4 = (f32[32]{0:T(128)S(1)}, f32[32]{0:T(128)S(1)}) all-reduce(f32[32]{0:T(128)S(1)} %reduce_sum.59, f32[32]{0:T(128)S(1)} %reduce_sum.61), channel_id=1, replica_groups=mesh['section'=4,'tm'=8] {'tm'}, use_global_device_ids=true, to_apply=%region_7.6 | all-reduce | flops 64 | bytes 512 | tf_op jit(solution)/shard_map/while/body/eval_jaxpr/while/body/eval_jaxpr/psum | solution.py:54
  247.5 6.6 %collective-permute-done.2 = bf16[4,64,256]{2,1,0:T(8,128)(2,1)S(1)} collective-permute-done((bf16[4,64,256]{2,1,0:T(8,128)(2,1)S(1)}, bf16[4,64,256]{2,1,0:T(8,128)(2,1)S(1)}, u32[]{:S(2)}, u32[]{:S(2)}) %collective-permute-start.2) | collective-permute-done | bytes 131104 | tf_op jit(solution)/shard_map/while/body/eval_jaxpr/ppermute | solution.py:34
  255.0 1.9 collective-permute-start
  256.9 2.4 collective-permute-start.1
  261.9 33.5 %while.53 = (s32[]{:T(128)}, f32[4,68,256]{2,1,0:T(8,128)S(1)}, s32[]{:T(128)}, f32[2,256]{1,0:T(2,128)S(1)}, f32[2,256]{1,0:T(2,128)S(1)}, /*index=5*/bf16[2,3,...) while((s32[]{:T(128)}, f32[4,68,256]{2,1,0:T(8,128)S(1)}, s32[]{:T(128)}, ...), condition=%wide.region_8.8_spmd.clone, body=%wide.region_1.7_spmd.clone.sunk | while | flops 322453952 | bytes 15810317 | solution.py:93
  262.4 12.0 %all-reduce.4 = (f32[32]{0:T(128)S(1)}, f32[32]{0:T(128)S(1)}) all-reduce(f32[32]{0:T(128)S(1)} %reduce_sum.59, f32[32]{0:T(128)S(1)} %reduce_sum.61), channel_id=1, replica_groups=mesh['section'=4,'tm'=8] {'tm'}, use_global_device_ids=true, to_apply=%region_7.6 | all-reduce | flops 64 | bytes 512 | tf_op jit(solution)/shard_map/while/body/eval_jaxpr/while/body/eval_jaxpr/psum | solution.py:54
  279.2 11.8 %all-reduce.4 = (f32[32]{0:T(128)S(1)}, f32[32]{0:T(128)S(1)}) all-reduce(f32[32]{0:T(128)S(1)} %reduce_sum.59, f32[32]{0:T(128)S(1)} %reduce_sum.61), channel_id=1, replica_groups=mesh['section'=4,'tm'=8] {'tm'}, use_global_device_ids=true, to_apply=%region_7.6 | all-reduce | flops 64 | bytes 512 | tf_op jit(solution)/shard_map/while/body/eval_jaxpr/while/body/eval_jaxpr/psum | solution.py:54
  297.4 6.6 %collective-permute-done.2 = bf16[4,64,256]{2,1,0:T(8,128)(2,1)S(1)} collective-permute-done((bf16[4,64,256]{2,1,0:T(8,128)(2,1)S(1)}, bf16[4,64,256]{2,1,0:T(8,128)(2,1)S(1)}, u32[]{:S(2)}, u32[]{:S(2)}) %collective-permute-start.2) | collective-permute-done | bytes 131104 | tf_op jit(solution)/shard_map/while/body/eval_jaxpr/ppermute | solution.py:34
  304.9 1.9 collective-permute-start
  306.8 2.4 collective-permute-start.1
  311.8 33.5 %while.53 = (s32[]{:T(128)}, f32[4,68,256]{2,1,0:T(8,128)S(1)}, s32[]{:T(128)}, f32[2,256]{1,0:T(2,128)S(1)}, f32[2,256]{1,0:T(2,128)S(1)}, /*index=5*/bf16[2,3,...) while((s32[]{:T(128)}, f32[4,68,256]{2,1,0:T(8,128)S(1)}, s32[]{:T(128)}, ...), condition=%wide.region_8.8_spmd.clone, body=%wide.region_1.7_spmd.clone.sunk | while | flops 322453952 | bytes 15810317 | solution.py:93
  312.3 12.0 %all-reduce.4 = (f32[32]{0:T(128)S(1)}, f32[32]{0:T(128)S(1)}) all-reduce(f32[32]{0:T(128)S(1)} %reduce_sum.59, f32[32]{0:T(128)S(1)} %reduce_sum.61), channel_id=1, replica_groups=mesh['section'=4,'tm'=8] {'tm'}, use_global_device_ids=true, to_apply=%region_7.6 | all-reduce | flops 64 | bytes 512 | tf_op jit(solution)/shard_map/while/body/eval_jaxpr/while/body/eval_jaxpr/psum | solution.py:54
  329.2 11.8 %all-reduce.4 = (f32[32]{0:T(128)S(1)}, f32[32]{0:T(128)S(1)}) all-reduce(f32[32]{0:T(128)S(1)} %reduce_sum.59, f32[32]{0:T(128)S(1)} %reduce_sum.61), channel_id=1, replica_groups=mesh['section'=4,'tm'=8] {'tm'}, use_global_device_ids=true, to_apply=%region_7.6 | all-reduce | flops 64 | bytes 512 | tf_op jit(solution)/shard_map/while/body/eval_jaxpr/while/body/eval_jaxpr/psum | solution.py:54
  347.3 6.6 %collective-permute-done.2 = bf16[4,64,256]{2,1,0:T(8,128)(2,1)S(1)} collective-permute-done((bf16[4,64,256]{2,1,0:T(8,128)(2,1)S(1)}, bf16[4,64,256]{2,1,0:T(8,128)(2,1)S(1)}, u32[]{:S(2)}, u32[]{:S(2)}) %collective-permute-start.2) | collective-permute-done | bytes 131104 | tf_op jit(solution)/shard_map/while/body/eval_jaxpr/ppermute | solution.py:34
  (591 shorter events, 100.2 us)
Async XLA Ops:
  0.0 4.0 %copy-start = (bf16[1,256,256]{2,1,0:T(8,128)(2,1)S(1)}, bf16[1,256,256]{2,1,0:T(8,128)(2,1)}, u32[]{:S(2)}) copy-start(bf16[1,256,256]{2,1,0:T(8,128)(2,1)} %param.19) | copy-start | bytes 393220
  0.0 5.0 %copy-start.1 = (f32[1,2,256]{2,1,0:T(2,128)S(1)}, f32[1,2,256]{2,1,0:T(2,128)}, u32[]{:S(2)}) copy-start(f32[1,2,256]{2,1,0:T(2,128)} %param.16) | copy-start | bytes 6148
  0.0 5.0 %copy-start.2 = (f32[1,2,256]{2,1,0:T(2,128)S(1)}, f32[1,2,256]{2,1,0:T(2,128)}, u32[]{:S(2)}) copy-start(f32[1,2,256]{2,1,0:T(2,128)} %param.17) | copy-start | bytes 6148
  6.0 5.3 %collective-permute-start = (bf16[4,2,256]{2,1,0:T(2,128)(2,1)S(1)}, bf16[4,2,256]{2,1,0:T(2,128)(2,1)S(1)}, u32[]{:S(2)}, u32[]{:S(2)}) collective-permute-start(bf16[4,2,256]{2,1,0:T(2,128)(2,1)S(1)} %get-tuple-element.702), channel_id=1, source_target_pairs={{1,0},{2,1},{3,2},{4,3},{5,4},{6,5},{7,6},{9,8},{10,9},{11,10},{12... | collective-permute-start | bytes 12296 | tf_op jit(solution)/shard_map/while/body/eval_jaxpr/ppermute | solution.py:24
  8.0 4.9 %collective-permute-start.1 = (bf16[4,2,256]{2,1,0:T(2,128)(2,1)S(1)}, bf16[4,2,256]{2,1,0:T(2,128)(2,1)S(1)}, u32[]{:S(2)}, u32[]{:S(2)}) collective-permute-start(bf16[4,2,256]{2,1,0:T(2,128)(2,1)S(1)} %get-tuple-element.703), channel_id=1, source_target_pairs={{0,1},{1,2},{2,3},{3,4},{4,5},{5,6},{6,7},{8,9},{9,10},{10,11},{11... | collective-permute-start | bytes 12296 | tf_op jit(solution)/shard_map/while/body/eval_jaxpr/ppermute | solution.py:22
  46.6 7.9 %collective-permute-start.2 = (bf16[4,64,256]{2,1,0:T(8,128)(2,1)S(1)}, bf16[4,64,256]{2,1,0:T(8,128)(2,1)S(1)}, u32[]{:S(2)}, u32[]{:S(2)}) collective-permute-start(bf16[4,64,256]{2,1,0:T(8,128)(2,1)S(1)} %get-tuple-element.705), channel_id=1, source_target_pairs={{0,8},{8,16},{16,24},{1,9},{9,17},{17,25},{2,10},{10,18},{18,26},{... | collective-permute-start | bytes 393224 | tf_op jit(solution)/shard_map/while/body/eval_jaxpr/ppermute | solution.py:34
  55.4 5.3 %collective-permute-start = (bf16[4,2,256]{2,1,0:T(2,128)(2,1)S(1)}, bf16[4,2,256]{2,1,0:T(2,128)(2,1)S(1)}, u32[]{:S(2)}, u32[]{:S(2)}) collective-permute-start(bf16[4,2,256]{2,1,0:T(2,128)(2,1)S(1)} %get-tuple-element.702), channel_id=1, source_target_pairs={{1,0},{2,1},{3,2},{4,3},{5,4},{6,5},{7,6},{9,8},{10,9},{11,10},{12... | collective-permute-start | bytes 12296 | tf_op jit(solution)/shard_map/while/body/eval_jaxpr/ppermute | solution.py:24
  57.3 4.9 %collective-permute-start.1 = (bf16[4,2,256]{2,1,0:T(2,128)(2,1)S(1)}, bf16[4,2,256]{2,1,0:T(2,128)(2,1)S(1)}, u32[]{:S(2)}, u32[]{:S(2)}) collective-permute-start(bf16[4,2,256]{2,1,0:T(2,128)(2,1)S(1)} %get-tuple-element.703), channel_id=1, source_target_pairs={{0,1},{1,2},{2,3},{3,4},{4,5},{5,6},{6,7},{8,9},{9,10},{10,11},{11... | collective-permute-start | bytes 12296 | tf_op jit(solution)/shard_map/while/body/eval_jaxpr/ppermute | solution.py:22
  96.5 7.9 %collective-permute-start.2 = (bf16[4,64,256]{2,1,0:T(8,128)(2,1)S(1)}, bf16[4,64,256]{2,1,0:T(8,128)(2,1)S(1)}, u32[]{:S(2)}, u32[]{:S(2)}) collective-permute-start(bf16[4,64,256]{2,1,0:T(8,128)(2,1)S(1)} %get-tuple-element.705), channel_id=1, source_target_pairs={{0,8},{8,16},{16,24},{1,9},{9,17},{17,25},{2,10},{10,18},{18,26},{... | collective-permute-start | bytes 393224 | tf_op jit(solution)/shard_map/while/body/eval_jaxpr/ppermute | solution.py:34
  105.3 5.3 %collective-permute-start = (bf16[4,2,256]{2,1,0:T(2,128)(2,1)S(1)}, bf16[4,2,256]{2,1,0:T(2,128)(2,1)S(1)}, u32[]{:S(2)}, u32[]{:S(2)}) collective-permute-start(bf16[4,2,256]{2,1,0:T(2,128)(2,1)S(1)} %get-tuple-element.702), channel_id=1, source_target_pairs={{1,0},{2,1},{3,2},{4,3},{5,4},{6,5},{7,6},{9,8},{10,9},{11,10},{12... | collective-permute-start | bytes 12296 | tf_op jit(solution)/shard_map/while/body/eval_jaxpr/ppermute | solution.py:24
  107.2 4.9 %collective-permute-start.1 = (bf16[4,2,256]{2,1,0:T(2,128)(2,1)S(1)}, bf16[4,2,256]{2,1,0:T(2,128)(2,1)S(1)}, u32[]{:S(2)}, u32[]{:S(2)}) collective-permute-start(bf16[4,2,256]{2,1,0:T(2,128)(2,1)S(1)} %get-tuple-element.703), channel_id=1, source_target_pairs={{0,1},{1,2},{2,3},{3,4},{4,5},{5,6},{6,7},{8,9},{9,10},{10,11},{11... | collective-permute-start | bytes 12296 | tf_op jit(solution)/shard_map/while/body/eval_jaxpr/ppermute | solution.py:22
  146.4 7.9 %collective-permute-start.2 = (bf16[4,64,256]{2,1,0:T(8,128)(2,1)S(1)}, bf16[4,64,256]{2,1,0:T(8,128)(2,1)S(1)}, u32[]{:S(2)}, u32[]{:S(2)}) collective-permute-start(bf16[4,64,256]{2,1,0:T(8,128)(2,1)S(1)} %get-tuple-element.705), channel_id=1, source_target_pairs={{0,8},{8,16},{16,24},{1,9},{9,17},{17,25},{2,10},{10,18},{18,26},{... | collective-permute-start | bytes 393224 | tf_op jit(solution)/shard_map/while/body/eval_jaxpr/ppermute | solution.py:34
  155.2 5.3 %collective-permute-start = (bf16[4,2,256]{2,1,0:T(2,128)(2,1)S(1)}, bf16[4,2,256]{2,1,0:T(2,128)(2,1)S(1)}, u32[]{:S(2)}, u32[]{:S(2)}) collective-permute-start(bf16[4,2,256]{2,1,0:T(2,128)(2,1)S(1)} %get-tuple-element.702), channel_id=1, source_target_pairs={{1,0},{2,1},{3,2},{4,3},{5,4},{6,5},{7,6},{9,8},{10,9},{11,10},{12... | collective-permute-start | bytes 12296 | tf_op jit(solution)/shard_map/while/body/eval_jaxpr/ppermute | solution.py:24
  157.1 4.9 %collective-permute-start.1 = (bf16[4,2,256]{2,1,0:T(2,128)(2,1)S(1)}, bf16[4,2,256]{2,1,0:T(2,128)(2,1)S(1)}, u32[]{:S(2)}, u32[]{:S(2)}) collective-permute-start(bf16[4,2,256]{2,1,0:T(2,128)(2,1)S(1)} %get-tuple-element.703), channel_id=1, source_target_pairs={{0,1},{1,2},{2,3},{3,4},{4,5},{5,6},{6,7},{8,9},{9,10},{10,11},{11... | collective-permute-start | bytes 12296 | tf_op jit(solution)/shard_map/while/body/eval_jaxpr/ppermute | solution.py:22
  196.3 7.9 %collective-permute-start.2 = (bf16[4,64,256]{2,1,0:T(8,128)(2,1)S(1)}, bf16[4,64,256]{2,1,0:T(8,128)(2,1)S(1)}, u32[]{:S(2)}, u32[]{:S(2)}) collective-permute-start(bf16[4,64,256]{2,1,0:T(8,128)(2,1)S(1)} %get-tuple-element.705), channel_id=1, source_target_pairs={{0,8},{8,16},{16,24},{1,9},{9,17},{17,25},{2,10},{10,18},{18,26},{... | collective-permute-start | bytes 393224 | tf_op jit(solution)/shard_map/while/body/eval_jaxpr/ppermute | solution.py:34
  205.1 5.3 %collective-permute-start = (bf16[4,2,256]{2,1,0:T(2,128)(2,1)S(1)}, bf16[4,2,256]{2,1,0:T(2,128)(2,1)S(1)}, u32[]{:S(2)}, u32[]{:S(2)}) collective-permute-start(bf16[4,2,256]{2,1,0:T(2,128)(2,1)S(1)} %get-tuple-element.702), channel_id=1, source_target_pairs={{1,0},{2,1},{3,2},{4,3},{5,4},{6,5},{7,6},{9,8},{10,9},{11,10},{12... | collective-permute-start | bytes 12296 | tf_op jit(solution)/shard_map/while/body/eval_jaxpr/ppermute | solution.py:24
  207.0 4.9 %collective-permute-start.1 = (bf16[4,2,256]{2,1,0:T(2,128)(2,1)S(1)}, bf16[4,2,256]{2,1,0:T(2,128)(2,1)S(1)}, u32[]{:S(2)}, u32[]{:S(2)}) collective-permute-start(bf16[4,2,256]{2,1,0:T(2,128)(2,1)S(1)} %get-tuple-element.703), channel_id=1, source_target_pairs={{0,1},{1,2},{2,3},{3,4},{4,5},{5,6},{6,7},{8,9},{9,10},{10,11},{11... | collective-permute-start | bytes 12296 | tf_op jit(solution)/shard_map/while/body/eval_jaxpr/ppermute | solution.py:22
  246.2 7.9 %collective-permute-start.2 = (bf16[4,64,256]{2,1,0:T(8,128)(2,1)S(1)}, bf16[4,64,256]{2,1,0:T(8,128)(2,1)S(1)}, u32[]{:S(2)}, u32[]{:S(2)}) collective-permute-start(bf16[4,64,256]{2,1,0:T(8,128)(2,1)S(1)} %get-tuple-element.705), channel_id=1, source_target_pairs={{0,8},{8,16},{16,24},{1,9},{9,17},{17,25},{2,10},{10,18},{18,26},{... | collective-permute-start | bytes 393224 | tf_op jit(solution)/shard_map/while/body/eval_jaxpr/ppermute | solution.py:34
  255.0 5.3 %collective-permute-start = (bf16[4,2,256]{2,1,0:T(2,128)(2,1)S(1)}, bf16[4,2,256]{2,1,0:T(2,128)(2,1)S(1)}, u32[]{:S(2)}, u32[]{:S(2)}) collective-permute-start(bf16[4,2,256]{2,1,0:T(2,128)(2,1)S(1)} %get-tuple-element.702), channel_id=1, source_target_pairs={{1,0},{2,1},{3,2},{4,3},{5,4},{6,5},{7,6},{9,8},{10,9},{11,10},{12... | collective-permute-start | bytes 12296 | tf_op jit(solution)/shard_map/while/body/eval_jaxpr/ppermute | solution.py:24
  256.9 4.9 %collective-permute-start.1 = (bf16[4,2,256]{2,1,0:T(2,128)(2,1)S(1)}, bf16[4,2,256]{2,1,0:T(2,128)(2,1)S(1)}, u32[]{:S(2)}, u32[]{:S(2)}) collective-permute-start(bf16[4,2,256]{2,1,0:T(2,128)(2,1)S(1)} %get-tuple-element.703), channel_id=1, source_target_pairs={{0,1},{1,2},{2,3},{3,4},{4,5},{5,6},{6,7},{8,9},{9,10},{10,11},{11... | collective-permute-start | bytes 12296 | tf_op jit(solution)/shard_map/while/body/eval_jaxpr/ppermute | solution.py:22
  296.1 7.9 %collective-permute-start.2 = (bf16[4,64,256]{2,1,0:T(8,128)(2,1)S(1)}, bf16[4,64,256]{2,1,0:T(8,128)(2,1)S(1)}, u32[]{:S(2)}, u32[]{:S(2)}) collective-permute-start(bf16[4,64,256]{2,1,0:T(8,128)(2,1)S(1)} %get-tuple-element.705), channel_id=1, source_target_pairs={{0,8},{8,16},{16,24},{1,9},{9,17},{17,25},{2,10},{10,18},{18,26},{... | collective-permute-start | bytes 393224 | tf_op jit(solution)/shard_map/while/body/eval_jaxpr/ppermute | solution.py:34
  304.9 5.3 %collective-permute-start = (bf16[4,2,256]{2,1,0:T(2,128)(2,1)S(1)}, bf16[4,2,256]{2,1,0:T(2,128)(2,1)S(1)}, u32[]{:S(2)}, u32[]{:S(2)}) collective-permute-start(bf16[4,2,256]{2,1,0:T(2,128)(2,1)S(1)} %get-tuple-element.702), channel_id=1, source_target_pairs={{1,0},{2,1},{3,2},{4,3},{5,4},{6,5},{7,6},{9,8},{10,9},{11,10},{12... | collective-permute-start | bytes 12296 | tf_op jit(solution)/shard_map/while/body/eval_jaxpr/ppermute | solution.py:24
  306.8 4.9 %collective-permute-start.1 = (bf16[4,2,256]{2,1,0:T(2,128)(2,1)S(1)}, bf16[4,2,256]{2,1,0:T(2,128)(2,1)S(1)}, u32[]{:S(2)}, u32[]{:S(2)}) collective-permute-start(bf16[4,2,256]{2,1,0:T(2,128)(2,1)S(1)} %get-tuple-element.703), channel_id=1, source_target_pairs={{0,1},{1,2},{2,3},{3,4},{4,5},{5,6},{6,7},{8,9},{9,10},{10,11},{11... | collective-permute-start | bytes 12296 | tf_op jit(solution)/shard_map/while/body/eval_jaxpr/ppermute | solution.py:22
  346.0 7.9 %collective-permute-start.2 = (bf16[4,64,256]{2,1,0:T(8,128)(2,1)S(1)}, bf16[4,64,256]{2,1,0:T(8,128)(2,1)S(1)}, u32[]{:S(2)}, u32[]{:S(2)}) collective-permute-start(bf16[4,64,256]{2,1,0:T(8,128)(2,1)S(1)} %get-tuple-element.705), channel_id=1, source_target_pairs={{0,8},{8,16},{16,24},{1,9},{9,17},{17,25},{2,10},{10,18},{18,26},{... | collective-permute-start | bytes 393224 | tf_op jit(solution)/shard_map/while/body/eval_jaxpr/ppermute | solution.py:34
where the time goes:
time: 357 us; the launch traced here: 354 us
  blocking collectives  166 us (46%)
  waiting for transfers between devices  56.9 us (16%)
  local copies, waits for them, and re-layouts  40.3 us (11%)
  starting transfers between devices  39.2 us (11%)
  matrix products  24.2 us (7%)
  other arithmetic  23.7 us (7%)
    psum x14, blocking collectives, group_act(): total, square = lax.psum((total, square), 'tm')  166 us
    ppermute x7, waiting for transfers between devices, shifted(): return lax.ppermute(block, axis, route)  46 us
    dot_general x126, matrix products, conv_same(): jnp.dot(window, weight[i, j], preferred_element_type=jnp.float32)  24 us
    squeeze x14, local copies, waits for them, and re-layouts, layer_deep(): kernel = lax.dynamic_index_in_dim(weights, layer, 0, keepdims=False)  18.9 us
    ppermute x7, starting transfers between devices, extended(): lax.ppermute(tail, axis, [(i, (i + 1) % count) for i in range(ends)])  16.8 us
    ppermute x7, starting transfers between devices, extended(): lax.ppermute(head, axis, [((i + 1) % count, i) for i in range(ends)])  13.4 us
    ppermute x7, waiting for transfers between devices, extended(): lax.ppermute(tail, axis, [(i, (i + 1) % count) for i in range(ends)])  10.9 us
    ppermute x7, starting transfers between devices, shifted(): return lax.ppermute(block, axis, route)  8.96 us
  transfers between devices with their start and end apart: 21, of which 14 were waited for; matrix products, arithmetic and copies ran while one was open for 2% of the time, Pallas kernels for 0%

commit v1 on v0

v1 whole, which is shorter than its diff:
```python
import functools
import math

import jax
import jax.numpy as jnp
from jax import lax
from jax.experimental import pallas as pl
from jax.experimental.pallas import tpu as pltpu
from jax.sharding import PartitionSpec as P

GROUPS = 32
STEPS = 1000
MESH = pl.DeviceIdType.MESH


def prepare(clean, noise, timestep, lift):
    chans = lift.shape[0]
    steps_f = timestep.astype(jnp.float32)
    level = jnp.cos(math.pi / 2.0 * (steps_f / STEPS + 0.008) / 1.008) ** 2
    noisy = jnp.sqrt(level)[:, None, None] * clean + jnp.sqrt(1.0 - level)[:, None, None] * noise
    lifted = (noisy[..., None] * lift).astype(jnp.bfloat16)
    half = chans // 2
    freqs = jnp.exp(-math.log(10000.0) * jnp.arange(half, dtype=jnp.float32) / half)
    angles = steps_f[:, None] * freqs[None, :]
    emb = jnp.concatenate([jnp.sin(angles), jnp.cos(angles)], axis=1).astype(jnp.bfloat16)
    return (lifted, emb)


def silu(z):
    half = 0.5 * z
    return half + half * jnp.tanh(half)


def kernel(
    dims,
    lifted,
    temb,
    gains,
    biases,
    weights,
    out,
    w,
    xin,
    hmid,
    staged,
    act3,
    st_send,
    st_recv,
    edge_send,
    edge_recv,
    st_ssem,
    st_rsem,
    edge_ssem,
    edge_rsem,
    blk_ssem,
    blk_rsem,
    w_sem,
    out_sem,
):
    n_time, n_section, micros, rows_f, frames, chans, layers = dims
    rows = rows_f * frames
    positions = rows * n_time
    width = chans // GROUPS
    count = positions * width
    sec = lax.axis_index("section")
    tm = lax.axis_index("tm")
    deep = sec < n_section // 2
    first = sec == 0
    last = sec == n_section - 1
    has_left = tm > 0
    has_right = tm < n_time - 1
    up = jnp.minimum(sec + 1, n_section - 1)
    down = jnp.maximum(sec - 1, 0)
    short = n_time <= 8

    def load_w(layer):
        return pltpu.make_async_copy(weights.at[layer], w.at[layer], w_sem.at[layer])

    load_w(0).start()

    @pl.when(deep)
    def _():
        for layer in range(1, layers):
            load_w(layer).start()

    barrier = pltpu.get_barrier_semaphore()

    def peers(section, begin):
        def one(r, carry):
            pl.semaphore_signal(
                barrier,
                inc=1,
                device_id=(section, lax.rem(tm + r, n_time)),
                device_id_type=MESH,
            )
            return carry

        lax.fori_loop(begin, n_time, one, 0, unroll=short)

    peers(sec, 1)

    @pl.when(jnp.logical_not(last))
    def _():
        peers(up, 0)

    @pl.when(jnp.logical_not(first))
    def _():
        peers(down, 0)

    def x_load(m):
        return pltpu.make_async_copy(lifted.at[m], xin.at[m], blk_rsem.at[m])

    @pl.when(first)
    def _():
        for m in range(micros):
            x_load(m).start()

    act3[0:frames, :] = jnp.zeros((frames, 3 * chans), jnp.bfloat16)
    act3[rows + frames : rows + 2 * frames, :] = jnp.zeros((frames, 3 * chans), jnp.bfloat16)

    def summarize(m, kind, value):
        st_send[m, kind, :, 0:chans] = jnp.sum(value, axis=0, keepdims=True)
        st_send[m, kind, :, chans : 2 * chans] = jnp.sum(value * value, axis=0, keepdims=True)
        for f in range(rows_f):
            edge_send[m, kind, 0, f : f + 1, :] = value[f * frames : f * frames + 1]
            edge_send[m, kind, 1, f : f + 1, :] = value[(f + 1) * frames - 1 : (f + 1) * frames]

    def edge_copy(m, kind, slot, side, section, peer):
        return pltpu.make_async_remote_copy(
            src_ref=edge_send.at[m, kind, side],
            dst_ref=edge_recv.at[m, slot, 1 - side],
            send_sem=edge_ssem.at[m, kind, side],
            recv_sem=edge_rsem.at[m, slot, 1 - side],
            device_id=(section, peer),
            device_id_type=MESH,
        )

    def publish(m, kind, slot, section, begin):
        def one(r, carry):
            pltpu.make_async_remote_copy(
                src_ref=st_send.at[m, kind],
                dst_ref=st_recv.at[m, slot, tm],
                send_sem=st_ssem.at[m, kind],
                recv_sem=st_rsem.at[m, slot],
                device_id=(section, lax.rem(tm + r, n_time)),
                device_id_type=MESH,
            ).start()
            return carry

        lax.fori_loop(begin, n_time, one, 0, unroll=short)
        if begin:
            st_recv[m, slot, tm] = st_send[m, kind]

        @pl.when(has_left)
        def _():
            edge_copy(m, kind, slot, 0, section, jnp.maximum(tm - 1, 0)).start()

        @pl.when(has_right)
        def _():
            edge_copy(m, kind, slot, 1, section, jnp.minimum(tm + 1, n_time - 1)).start()

    def drain(m, kind, begin):
        whole = st_recv.at[m, 0, pl.ds(0, n_time - begin)]
        pltpu.make_async_copy(whole, whole, st_ssem.at[m, kind]).wait()

        @pl.when(has_left)
        def _():
            pltpu.make_async_copy(
                edge_send.at[m, kind, 0], edge_send.at[m, kind, 0], edge_ssem.at[m, kind, 0]
            ).wait()

        @pl.when(has_right)
        def _():
            pltpu.make_async_copy(
                edge_send.at[m, kind, 1], edge_send.at[m, kind, 1], edge_ssem.at[m, kind, 1]
            ).wait()

    def await_stats(m, slot, begin):
        whole = st_recv.at[m, slot, pl.ds(0, n_time - begin)]
        pltpu.make_async_copy(whole, whole, st_rsem.at[m, slot]).wait()

    def await_edges(m, slot):
        @pl.when(has_left)
        def _():
            pltpu.make_async_copy(
                edge_recv.at[m, slot, 0], edge_recv.at[m, slot, 0], edge_rsem.at[m, slot, 0]
            ).wait()

        @pl.when(has_right)
        def _():
            pltpu.make_async_copy(
                edge_recv.at[m, slot, 1], edge_recv.at[m, slot, 1], edge_rsem.at[m, slot, 1]
            ).wait()

    lanes = lax.broadcasted_iota(jnp.int32, (8, 2 * chans), 1)

    def group_total(pair):
        total = jnp.broadcast_to(pair, (8, 2 * chans))
        step = 1
        while step < width:
            ahead = pltpu.roll(total, 2 * chans - step, 1)
            behind = pltpu.roll(total, step, 1)
            total = total + jnp.where((lanes // step) % 2 == 0, ahead, behind)
            step *= 2
        return total[0:1]

    def convolve(m, slot, layer, hidden, shift_row):
        stats = jnp.sum(st_recv[m, slot], axis=0)
        s1 = stats[:, 0:chans]
        s2 = stats[:, chans : 2 * chans]
        if shift_row is not None:
            s2 = s2 + 2.0 * shift_row * s1 + positions * (shift_row * shift_row)
            s1 = s1 + positions * shift_row
        total = group_total(jnp.concatenate([s1, s2], axis=1))
        mean = total[:, 0:chans] / count
        var = total[:, chans : 2 * chans] / count - mean * mean
        scale = lax.rsqrt(var + 1e-05) * gains[layer]
        offset = biases[layer] - mean * scale
        act = silu(hidden * scale + offset)
        edges = edge_recv[m, slot]
        if shift_row is not None:
            edges = edges + shift_row
        edges = silu(edges * scale + offset)
        before = jnp.where(has_left, edges[0], 0.0)
        after = jnp.where(has_right, edges[1], 0.0)
        place = lax.broadcasted_iota(jnp.int32, (frames, chans), 0)
        for f in range(rows_f):
            part = act[f * frames : (f + 1) * frames]
            prev = jnp.where(place == 0, before[f : f + 1], pltpu.roll(part, 1, 0))
            nxt = jnp.where(place == frames - 1, after[f : f + 1], pltpu.roll(part, frames - 1, 0))
            at = slice((f + 1) * frames, (f + 2) * frames)
            act3[at, 0:chans] = prev.astype(jnp.bfloat16)
            act3[at, chans : 2 * chans] = part.astype(jnp.bfloat16)
            act3[at, 2 * chans : 3 * chans] = nxt.astype(jnp.bfloat16)
        total = hidden
        for i in range(3):
            total = total + jnp.dot(
                act3[i * frames : i * frames + rows],
                w[layer, i],
                preferred_element_type=jnp.float32,
            )
        return total

    def block_copy(m):
        return pltpu.make_async_remote_copy(
            src_ref=staged.at[m],
            dst_ref=xin.at[m],
            send_sem=blk_ssem.at[m],
            recv_sem=blk_rsem.at[m],
            device_id=(up, tm),
            device_id_type=MESH,
        )

    def out_copy(m):
        return pltpu.make_async_copy(staged.at[m], out.at[m], out_sem.at[m])

    def finish(m, hidden):
        rounded = hidden.astype(jnp.bfloat16)
        staged[m] = rounded

        @pl.when(jnp.logical_not(last))
        def _():
            summarize(m, 2, rounded.astype(jnp.float32))
            publish(m, 2, 0, up, 0)
            block_copy(m).start()

        out_copy(m).start()

    def enter(m):
        @pl.when(first)
        def _():
            await_stats(m, 0, 1)

        @pl.when(jnp.logical_not(first))
        def _():
            await_stats(m, 0, 0)
            pltpu.make_async_copy(xin.at[m], xin.at[m], blk_rsem.at[m]).wait()

        await_edges(m, 0)
        shift_row = temb[m]
        hidden = xin[m].astype(jnp.float32) + shift_row
        hidden = convolve(m, 0, 0, hidden, shift_row)

        @pl.when(deep)
        def _():
            hmid[m] = hidden
            summarize(m, 1, hidden)
            publish(m, 1, 1, sec, 1)

        @pl.when(jnp.logical_not(deep))
        def _():
            finish(m, hidden)

    def leave(m):
        @pl.when(deep)
        def _():
            await_stats(m, 1, 1)
            await_edges(m, 1)
            finish(m, convolve(m, 1, 1, hmid[m], None))

    @pl.when(first)
    def _():
        for m in range(micros):
            x_load(m).wait()
            summarize(m, 0, xin[m].astype(jnp.float32))

    arrivals = n_time - 1
    arrivals = arrivals + n_time * jnp.where(last, 0, 1) + n_time * jnp.where(first, 0, 1)
    pl.semaphore_wait(barrier, arrivals)

    @pl.when(first)
    def _():
        for m in range(micros):
            publish(m, 0, 0, sec, 1)

    load_w(0).wait()

    @pl.when(deep)
    def _():
        for layer in range(1, layers):
            load_w(layer).wait()

    enter(0)
    for m in range(1, micros):
        enter(m)
        leave(m - 1)
    leave(micros - 1)

    @pl.when(first)
    def _():
        for m in range(micros):
            drain(m, 0, 1)

    @pl.when(deep)
    def _():
        for m in range(micros):
            drain(m, 1, 1)

    @pl.when(jnp.logical_not(last))
    def _():
        for m in range(micros):
            drain(m, 2, 0)
            block_copy(m).wait_send()

    for m in range(micros):
        out_copy(m).wait()


def on_device(clean, noise, timestep, lift, norm_gain, norm_bias, conv_weight, time_proj):
    lifted, emb = prepare(clean, noise, timestep, lift)
    temb = jnp.dot(emb, time_proj[0], preferred_element_type=jnp.float32)
    n_time = lax.axis_size("tm")
    n_section = lax.axis_size("section")
    micros, rows_f, frames, chans = lifted.shape
    layers = norm_gain.shape[1]
    rows = rows_f * frames
    dims = (n_time, n_section, micros, rows_f, frames, chans, layers)
    vmem = pl.BlockSpec(memory_space=pltpu.VMEM)
    hbm = pl.BlockSpec(memory_space=pl.ANY)
    dma = pltpu.SemaphoreType.DMA
    saved = pl.pallas_call(
        functools.partial(kernel, dims),
        out_shape=jax.ShapeDtypeStruct((micros, rows, chans), jnp.bfloat16),
        in_specs=[hbm, vmem, vmem, vmem, hbm],
        out_specs=hbm,
        scratch_shapes=[
            pltpu.VMEM((layers, 3, 3 * chans, chans), jnp.bfloat16),
            pltpu.VMEM((micros, rows, chans), jnp.bfloat16),
            pltpu.VMEM((micros, rows, chans), jnp.float32),
            pltpu.VMEM((micros, rows, chans), jnp.bfloat16),
            pltpu.VMEM((rows + 2 * frames, 3 * chans), jnp.bfloat16),
            pltpu.VMEM((micros, 3, 1, 2 * chans), jnp.float32),
            pltpu.VMEM((micros, 2, n_time, 1, 2 * chans), jnp.float32),
            pltpu.VMEM((micros, 3, 2, rows_f, chans), jnp.float32),
            pltpu.VMEM((micros, 2, 2, rows_f, chans), jnp.float32),
            dma((micros, 3)),
            dma((micros, 2)),
            dma((micros, 3, 2)),
            dma((micros, 2, 2)),
            dma((micros,)),
            dma((micros,)),
            dma((layers,)),
            dma((micros,)),
        ],
        compiler_params=pltpu.CompilerParams(collective_id=0, has_side_effects=True),
    )(
        lifted.reshape(micros, rows, chans),
        temb.reshape(micros, 1, chans),
        norm_gain.reshape(layers, 1, chans),
        norm_bias.reshape(layers, 1, chans),
        conv_weight.reshape(layers, 3, 3 * chans, chans),
    )
    return saved.reshape(1, micros, rows_f, frames, chans)


def solution(mesh):
    in_specs = (
        P(None, None, "tm"),
        P(None, None, "tm"),
        P(),
        P(),
        P("section", None, None),
        P("section", None, None),
        P("section", None, None, None, None, None),
        P("section", None, None),
    )
    out_specs = P("section", None, None, "tm", None)
    return jax.shard_map(
        on_device, mesh=mesh, in_specs=in_specs, out_specs=out_specs, check_vma=False
    )
```

time: 357 us -> 53.4 us (0.15)
  blocking collectives: 166 us -> 0 us
  waiting for transfers between devices: 56.9 us -> 0 us
  Pallas kernels: 0 us -> 43.7 us
  starting transfers between devices: 39.2 us -> 0 us
  local copies, waits for them, and re-layouts: 40.3 us -> 5.13 us
  matrix products: 24.2 us -> 0.14 us
  other arithmetic: 23.7 us -> 3.99 us
    psum x14 -> x0, blocking collectives: 166 us -> none  [group_act(): total, square = lax.psum((total, square), 'tm')]
    ppermute x21 -> x0, waiting for transfers between devices: 56.9 us -> none  [the longest x7 46 us: shifted(): return lax.ppermute(block, axis, route)]
    pallas_call x0 -> x1, Pallas kernels: none -> 43.7 us  [on_device(): pl.pallas_call(functools.partial(kernel, dims), out_shape=jax.ShapeDtypeS...]
    ppermute x21 -> x0, starting transfers between devices: 39.2 us -> none  [the longest x7 16.8 us: extended(): lax.ppermute(tail, axis, [(i, (i + 1) % count) for i in range(ends)])]
    dot_general x126 -> x0, matrix products: 24 us -> none  [conv_same(): jnp.dot(window, weight[i, j], preferred_element_type=jnp.float32)]
    squeeze x14 -> x0, local copies, waits for them, and re-layouts: 18.9 us -> none  [layer_deep(): kernel = lax.dynamic_index_in_dim(weights, layer, 0, keepdims=False)]
    select_n x35 -> x0, other arithmetic: 9.69 us -> none  [the longest x7 6.48 us: tick(): section_in = jnp.where(section_id == 0, first, inbox)]
    dynamic_slice x28 -> x0, local copies, waits for them, and re-layouts: 6.66 us -> none  [the longest x7 6.44 us: tick(): older = lax.dynamic_index_in_dim(saved, picked, 0, keepdims=False)]
  transfers between devices with their start and end apart: 21 -> 0, of which waited for: 14 -> 0; matrix products, arithmetic and copies ran while one was open for 2% -> 0% of each run, Pallas kernels for 0% -> 0%
where the time goes in v1:
time: 53.4 us; the launch traced here: 53 us
  Pallas kernels  43.7 us (82%)
  local copies, waits for them, and re-layouts  5.13 us (10%)
  other arithmetic  3.99 us (7%)
    pallas_call x1, Pallas kernels, on_device(): pl.pallas_call(functools.partial(kernel, dims), out_shape=jax.ShapeDtypeS...  43.7 us
    unnamed x3, local copies, waits for them, and re-layouts  1.89 us
    convert_element_type x1, other arithmetic, prepare(): lifted = (noisy[..., None] * lift).astype(jnp.bfloat16)  1.68 us
    reshape x1, local copies, waits for them, and re-layouts, on_device(): norm_gain.reshape(layers, 1, chans)  1.28 us
    reshape x1, local copies, waits for them, and re-layouts, on_device(): norm_bias.reshape(layers, 1, chans)  1.27 us

profile of v1, /device:TPU:26, one launch (start us, length us, event | category | flops | bytes accessed | tf_op | source)
XLA Modules:
  0.0 53.0 jit_solution(3289026126704672254)
XLA Ops:
  0.0 0.0 copy-start
  0.0 0.7 %convert_element_type.8 = f32[4]{0:T(128)S(1)} convert(s32[4]{0:T(128)} %param.10) | non-fusion elementwise | flops 4 | bytes 32 | tf_op jit(solution)/shard_map/convert_element_type | solution.py:18
  0.7 0.1 fusion.2
  0.8 0.7 %fusion.8 = (f32[4]{0:T(128)S(1)}, f32[4]{0:T(128)S(1)}) fusion(s32[4]{0:T(128)} %param.10), kind=kLoop, calls=%fused_computation.15 | loop fusion | flops 24 | bytes 48 | tf_op jit(solution)/shard_map/sqrt | solution.py:20
  1.5 0.0 copy-done
  1.5 0.1 fusion
  1.7 0.6 %reshape.28.temb = f32[4,1,256]{2,1,0:T(1,128)} reshape(f32[4,256]{1,0:T(4,128)S(1)} %fusion) | data formatting | bytes 8192 | tf_op jit(solution)/shard_map/reshape | solution.py:388
  2.3 1.3 %reshape.29.gains = f32[2,1,256]{2,1,0:T(1,128)} reshape(f32[1,2,256]{2,1,0:T(2,128)} %param.12) | data formatting | bytes 4096 | tf_op jit(solution)/shard_map/reshape | solution.py:389
  3.6 1.3 %reshape.30.biases = f32[2,1,256]{2,1,0:T(1,128)} reshape(f32[1,2,256]{2,1,0:T(2,128)} %param.13) | data formatting | bytes 4096 | tf_op jit(solution)/shard_map/reshape | solution.py:390
  4.8 0.8 %multiply_add_fusion = f32[4,4,64]{2,1,0:T(4,128)S(1)} fusion(f32[4,4,64]{2,1,0:T(4,128)} %param.9, f32[4,4,64]{2,1,0:T(4,128)} %param.8, f32[4]{0:T(128)S(1)} %get-tuple-element.8, f32[4]{0:T(128)S(1)} %get-tuple-element.7), kind=kLoop, calls=%fused_computation.3 | loop fusion | flops 3072 | bytes 12320 | tf_op jit(solution)/shard_map/add | solution.py:20
  5.6 0.1 mul.53
  5.7 1.7 %multiply_convert_fusion.lifted = bf16[4,256,256]{2,1,0:T(8,128)(2,1)} fusion(f32[256]{0:T(256)} %param.11, f32[4,256]{1,0:T(4,128)S(1)} %mul.53), kind=kLoop, calls=%fused_computation | loop fusion | flops 524288 | bytes 529408 | tf_op jit(solution)/shard_map/convert_element_type | solution.py:21
  7.4 43.7 %shard_map.82 = bf16[4,256,256]{2,1,0:T(8,128)(2,1)} custom-call(bf16[4,256,256]{2,1,0:T(8,128)(2,1)} %multiply_convert_fusion.lifted, f32[4,1,256]{2,1,0:T(1,128)} %reshape.28.temb, f32[2,1,256]{2,1,0:T(1,128)} %reshape.29.gains, f32[2,1,256]{2,1,0:T(1,128)} %reshape.30.biases, bf16[2,3,768,256]{3,2,1,0:T(8,128)(2,1)} %bitcast.5), custom_call_target="tpu_custom_call" | custom-call | tf_op jit(solution)/shard_map/pallas_call | solution.py:361
  51.1 1.9 %copy.10 = bf16[1,4,4,64,256]{4,3,2,1,0:T(8,128)(2,1)} copy(bf16[1,4,4,64,256]{4,3,2,1,0:T(8,128)(2,1)} %bitcast.6) | data formatting | bytes 1048576
  (1 shorter events, 0.0 us)
Async XLA Ops:
  0.0 1.5 %copy-start = (bf16[1,256,256]{2,1,0:T(8,128)(2,1)S(1)}, bf16[1,256,256]{2,1,0:T(8,128)(2,1)}, u32[]{:S(2)}) copy-start(bf16[1,256,256]{2,1,0:T(8,128)(2,1)} %param.15) | copy-start | bytes 393220

commit v2 on v1

--- a/solution.py
+++ b/solution.py
@@ -13,19 +13,6 @@
 MESH = pl.DeviceIdType.MESH
 
 
-def prepare(clean, noise, timestep, lift):
-    chans = lift.shape[0]
-    steps_f = timestep.astype(jnp.float32)
-    level = jnp.cos(math.pi / 2.0 * (steps_f / STEPS + 0.008) / 1.008) ** 2
-    noisy = jnp.sqrt(level)[:, None, None] * clean + jnp.sqrt(1.0 - level)[:, None, None] * noise
-    lifted = (noisy[..., None] * lift).astype(jnp.bfloat16)
-    half = chans // 2
-    freqs = jnp.exp(-math.log(10000.0) * jnp.arange(half, dtype=jnp.float32) / half)
-    angles = steps_f[:, None] * freqs[None, :]
-    emb = jnp.concatenate([jnp.sin(angles), jnp.cos(angles)], axis=1).astype(jnp.bfloat16)
-    return (lifted, emb)
-
-
 def silu(z):
     half = 0.5 * z
     return half + half * jnp.tanh(half)
@@ -33,16 +20,26 @@
 
 def kernel(
     dims,
-    lifted,
-    temb,
-    gains,
-    biases,
+    timestep,
+    clean_in,
+    noise_in,
+    lift_in,
+    gains_in,
+    biases_in,
+    proj_in,
     weights,
-    out,
+    staged,
     w,
     xin,
     hmid,
-    staged,
+    clean,
+    noise,
+    lift,
+    gains,
+    biases,
+    proj,
+    noisy,
+    temb,
     act3,
     st_send,
     st_recv,
@@ -55,7 +52,7 @@
     blk_ssem,
     blk_rsem,
     w_sem,
-    out_sem,
+    in_sem,
 ):
     n_time, n_section, micros, rows_f, frames, chans, layers = dims
     rows = rows_f * frames
@@ -76,12 +73,26 @@
     def load_w(layer):
         return pltpu.make_async_copy(weights.at[layer], w.at[layer], w_sem.at[layer])
 
-    load_w(0).start()
-
-    @pl.when(deep)
-    def _():
-        for layer in range(1, layers):
-            load_w(layer).start()
+    small = [
+        pltpu.make_async_copy(src, dst, in_sem.at[k])
+        for k, (src, dst) in enumerate(
+            [
+                (proj_in.at[0], proj),
+                (gains_in.at[0], gains),
+                (biases_in.at[0], biases),
+                (clean_in, clean),
+                (noise_in, noise),
+                (lift_in, lift),
+            ]
+        )
+    ]
+    for copy in small[:3]:
+        copy.start()
+
+    @pl.when(first)
+    def _():
+        for copy in small[3:]:
+            copy.start()
 
     barrier = pltpu.get_barrier_semaphore()
 
@@ -107,13 +118,12 @@
     def _():
         peers(down, 0)
 
-    def x_load(m):
-        return pltpu.make_async_copy(lifted.at[m], xin.at[m], blk_rsem.at[m])
-
-    @pl.when(first)
-    def _():
-        for m in range(micros):
-            x_load(m).start()
+    load_w(0).start()
+
+    @pl.when(deep)
+    def _():
+        for layer in range(1, layers):
+            load_w(layer).start()
 
     act3[0:frames, :] = jnp.zeros((frames, 3 * chans), jnp.bfloat16)
     act3[rows + frames : rows + 2 * frames, :] = jnp.zeros((frames, 3 * chans), jnp.bfloat16)
@@ -214,8 +224,8 @@
         total = group_total(jnp.concatenate([s1, s2], axis=1))
         mean = total[:, 0:chans] / count
         var = total[:, chans : 2 * chans] / count - mean * mean
-        scale = lax.rsqrt(var + 1e-05) * gains[layer]
-        offset = biases[layer] - mean * scale
+        scale = lax.rsqrt(var + 1e-05) * gains[layer : layer + 1, :]
+        offset = biases[layer : layer + 1, :] - mean * scale
         act = silu(hidden * scale + offset)
         edges = edge_recv[m, slot]
         if shift_row is not None:
@@ -251,9 +261,6 @@
             device_id_type=MESH,
         )
 
-    def out_copy(m):
-        return pltpu.make_async_copy(staged.at[m], out.at[m], out_sem.at[m])
-
     def finish(m, hidden):
         rounded = hidden.astype(jnp.bfloat16)
         staged[m] = rounded
@@ -264,8 +271,6 @@
             publish(m, 2, 0, up, 0)
             block_copy(m).start()
 
-        out_copy(m).start()
-
     def enter(m):
         @pl.when(first)
         def _():
@@ -277,7 +282,7 @@
             pltpu.make_async_copy(xin.at[m], xin.at[m], blk_rsem.at[m]).wait()
 
         await_edges(m, 0)
-        shift_row = temb[m]
+        shift_row = temb[m : m + 1, :]
         hidden = xin[m].astype(jnp.float32) + shift_row
         hidden = convolve(m, 0, 0, hidden, shift_row)
 
@@ -298,11 +303,42 @@
             await_edges(m, 1)
             finish(m, convolve(m, 1, 1, hmid[m], None))
 
+    half = chans // 2
+    slots = temb.shape[0]
+    which = lax.broadcasted_iota(jnp.int32, (slots, half), 0)
+    steps_f = jnp.zeros((slots, half), jnp.float32)
+    for m in range(micros):
+        steps_f = jnp.where(which == m, timestep[m].astype(jnp.float32), steps_f)
+
     @pl.when(first)
     def _():
-        for m in range(micros):
-            x_load(m).wait()
+        level = jnp.cos(math.pi / 2.0 * (steps_f / STEPS + 0.008) / 1.008) ** 2
+        keep = jnp.sqrt(level)
+        blur = jnp.sqrt(1.0 - level)
+        for copy in small[3:]:
+            copy.wait()
+        for m in range(micros):
+            noisy[m * rows_f : (m + 1) * rows_f, :] = (
+                keep[m : m + 1, 0:1] * clean[m] + blur[m : m + 1, 0:1] * noise[m]
+            )
+        columns = jnp.transpose(noisy[...])
+        for m in range(micros):
+            for f in range(rows_f):
+                at = m * rows_f + f
+                xin[m, f * frames : (f + 1) * frames, :] = (
+                    columns[:, at : at + 1] * lift[...]
+                ).astype(jnp.bfloat16)
             summarize(m, 0, xin[m].astype(jnp.float32))
+
+    order = lax.broadcasted_iota(jnp.int32, (slots, half), 1).astype(jnp.float32)
+    angles = steps_f * jnp.exp(-math.log(10000.0) * order / half)
+    for copy in small[:3]:
+        copy.wait()
+    temb[...] = jnp.dot(
+        jnp.sin(angles).astype(jnp.bfloat16), proj[0:half, :], preferred_element_type=jnp.float32
+    ) + jnp.dot(
+        jnp.cos(angles).astype(jnp.bfloat16), proj[half:chans, :], preferred_element_type=jnp.float32
+    )
 
     arrivals = n_time - 1
     arrivals = arrivals + n_time * jnp.where(last, 0, 1) + n_time * jnp.where(first, 0, 1)
@@ -342,17 +378,14 @@
             drain(m, 2, 0)
             block_copy(m).wait_send()
 
-    for m in range(micros):
-        out_copy(m).wait()
-
 
 def on_device(clean, noise, timestep, lift, norm_gain, norm_bias, conv_weight, time_proj):
-    lifted, emb = prepare(clean, noise, timestep, lift)
-    temb = jnp.dot(emb, time_proj[0], preferred_element_type=jnp.float32)
     n_time = lax.axis_size("tm")
     n_section = lax.axis_size("section")
-    micros, rows_f, frames, chans = lifted.shape
+    micros, rows_f, frames = clean.shape
+    chans = lift.shape[0]
     layers = norm_gain.shape[1]
+    slots = -(-micros // 8) * 8
     rows = rows_f * frames
     dims = (n_time, n_section, micros, rows_f, frames, chans, layers)
     vmem = pl.BlockSpec(memory_space=pltpu.VMEM)
@@ -361,13 +394,20 @@
     saved = pl.pallas_call(
         functools.partial(kernel, dims),
         out_shape=jax.ShapeDtypeStruct((micros, rows, chans), jnp.bfloat16),
-        in_specs=[hbm, vmem, vmem, vmem, hbm],
-        out_specs=hbm,
+        in_specs=[pl.BlockSpec(memory_space=pltpu.SMEM)] + [hbm] * 7,
+        out_specs=vmem,
         scratch_shapes=[
             pltpu.VMEM((layers, 3, 3 * chans, chans), jnp.bfloat16),
             pltpu.VMEM((micros, rows, chans), jnp.bfloat16),
             pltpu.VMEM((micros, rows, chans), jnp.float32),
-            pltpu.VMEM((micros, rows, chans), jnp.bfloat16),
+            pltpu.VMEM((micros, rows_f, frames), jnp.float32),
+            pltpu.VMEM((micros, rows_f, frames), jnp.float32),
+            pltpu.VMEM((1, chans), jnp.float32),
+            pltpu.VMEM((layers, chans), jnp.float32),
+            pltpu.VMEM((layers, chans), jnp.float32),
+            pltpu.VMEM((chans, chans), jnp.bfloat16),
+            pltpu.VMEM((micros * rows_f, frames), jnp.float32),
+            pltpu.VMEM((slots, chans), jnp.float32),
             pltpu.VMEM((rows + 2 * frames, 3 * chans), jnp.bfloat16),
             pltpu.VMEM((micros, 3, 1, 2 * chans), jnp.float32),
             pltpu.VMEM((micros, 2, n_time, 1, 2 * chans), jnp.float32),
@@ -380,14 +420,19 @@
             dma((micros,)),
             dma((micros,)),
             dma((layers,)),
-            dma((micros,)),
+            dma((6,)),
         ],
-        compiler_params=pltpu.CompilerParams(collective_id=0, has_side_effects=True),
+        compiler_params=pltpu.CompilerParams(
+            collective_id=0, has_side_effects=True
+        ),
     )(
-        lifted.reshape(micros, rows, chans),
-        temb.reshape(micros, 1, chans),
-        norm_gain.reshape(layers, 1, chans),
-        norm_bias.reshape(layers, 1, chans),
+        timestep,
+        clean,
+        noise,
+        lift.reshape(1, chans),
+        norm_gain,
+        norm_bias,
+        time_proj,
         conv_weight.reshape(layers, 3, 3 * chans, chans),
     )
     return saved.reshape(1, micros, rows_f, frames, chans)

time: 53.4 us -> 46 us (0.86)
  other arithmetic: 3.99 us -> 0 us
  local copies, waits for them, and re-layouts: 5.13 us -> 1.88 us
    reshape x3 -> x0, local copies, waits for them, and re-layouts: 3.16 us -> none  [the longest x1 1.28 us: on_device(): norm_gain.reshape(layers, 1, chans)]
    convert_element_type x2 -> x0, other arithmetic: 2.37 us -> none  [the longest x1 1.68 us: prepare(): lifted = (noisy[..., None] * lift).astype(jnp.bfloat16)]
    add x1 -> x0, other arithmetic: 0.79 us -> none  [prepare(): jnp.sqrt(level)[:, None, None] * clean]
    sqrt x1 -> x0, other arithmetic: 0.71 us -> none  [prepare(): jnp.sqrt(level)[:, None, None] * clean]
    unnamed x3 -> x1, local copies, waits for them, and re-layouts: 1.89 us -> 1.88 us
where the time goes in v2:
time: 46 us; the launch traced here: 45.9 us
  Pallas kernels  44 us (96%)
  local copies, waits for them, and re-layouts  1.88 us (4%)
    pallas_call x1, Pallas kernels, on_device(): pl.pallas_call(functools.partial(kernel, dims), out_shape=jax.ShapeDtypeS...  44 us
    unnamed x1, local copies, waits for them, and re-layouts  1.88 us

profile of v2, /device:TPU:26, one launch (start us, length us, event | category | flops | bytes accessed | tf_op | source)
XLA Modules:
  0.0 45.9 jit_solution(3835260291419338288)
XLA Ops:
  0.0 44.0 %shard_map.82 = bf16[4,256,256]{2,1,0:T(8,128)(2,1)} custom-call(s32[4]{0:T(128)} %timestep.1, f32[4,4,64]{2,1,0:T(4,128)} %clean_in.1, f32[4,4,64]{2,1,0:T(4,128)} %noise_in.1, f32[1,256]{1,0:T(1,128)} %bitcast.5, f32[1,2,256]{2,1,0:T(2,128)} %gains_in.1, f32[1,2,256]{2,1,0:T(2,128)} %biases_in.1, bf16[1,256,256]{2,1,0:T(8,128)(2,1)} %proj_in.1, ...), custom_call_target="tpu_custom_call" | custom-call | tf_op jit(solution)/shard_map/pallas_call | solution.py:394
  44.0 1.9 %copy.10 = bf16[1,4,4,64,256]{4,3,2,1,0:T(8,128)(2,1)} copy(bf16[1,4,4,64,256]{4,3,2,1,0:T(8,128)(2,1)} %bitcast.4) | data formatting | bytes 1048576

commit v3 on v2

--- a/solution.py
+++ b/solution.py
@@ -20,7 +20,7 @@
 
 def kernel(
     dims,
-    timestep,
+    steps_in,
     clean_in,
     noise_in,
     lift_in,
@@ -40,6 +40,7 @@
     proj,
     noisy,
     temb,
+    timestep,
     act3,
     st_send,
     st_recv,
@@ -77,6 +78,7 @@
         pltpu.make_async_copy(src, dst, in_sem.at[k])
         for k, (src, dst) in enumerate(
             [
+                (steps_in, timestep),
                 (proj_in.at[0], proj),
                 (gains_in.at[0], gains),
                 (biases_in.at[0], biases),
@@ -86,12 +88,12 @@
             ]
         )
     ]
-    for copy in small[:3]:
+    for copy in small[:4]:
         copy.start()
 
     @pl.when(first)
     def _():
-        for copy in small[3:]:
+        for copy in small[4:]:
             copy.start()
 
     barrier = pltpu.get_barrier_semaphore()
@@ -108,15 +110,11 @@
 
         lax.fori_loop(begin, n_time, one, 0, unroll=short)
 
+    @pl.when(jnp.logical_not(first))
+    def _():
+        peers(down, 0)
+
     peers(sec, 1)
-
-    @pl.when(jnp.logical_not(last))
-    def _():
-        peers(up, 0)
-
-    @pl.when(jnp.logical_not(first))
-    def _():
-        peers(down, 0)
 
     load_w(0).start()
 
@@ -124,9 +122,6 @@
     def _():
         for layer in range(1, layers):
             load_w(layer).start()
-
-    act3[0:frames, :] = jnp.zeros((frames, 3 * chans), jnp.bfloat16)
-    act3[rows + frames : rows + 2 * frames, :] = jnp.zeros((frames, 3 * chans), jnp.bfloat16)
 
     def summarize(m, kind, value):
         st_send[m, kind, :, 0:chans] = jnp.sum(value, axis=0, keepdims=True)
@@ -238,18 +233,26 @@
             part = act[f * frames : (f + 1) * frames]
             prev = jnp.where(place == 0, before[f : f + 1], pltpu.roll(part, 1, 0))
             nxt = jnp.where(place == frames - 1, after[f : f + 1], pltpu.roll(part, frames - 1, 0))
-            at = slice((f + 1) * frames, (f + 2) * frames)
+            at = slice(f * frames, (f + 1) * frames)
             act3[at, 0:chans] = prev.astype(jnp.bfloat16)
             act3[at, chans : 2 * chans] = part.astype(jnp.bfloat16)
             act3[at, 2 * chans : 3 * chans] = nxt.astype(jnp.bfloat16)
-        total = hidden
-        for i in range(3):
-            total = total + jnp.dot(
-                act3[i * frames : i * frames + rows],
-                w[layer, i],
-                preferred_element_type=jnp.float32,
+        above, level, below = (
+            jnp.dot(act3[span], w[layer, i], preferred_element_type=jnp.float32)
+            for i, span in enumerate(
+                (slice(0, rows - frames), slice(0, rows), slice(frames, rows))
             )
-        return total
+        )
+        level = hidden + level
+        inner = slice(frames, rows - frames)
+        return jnp.concatenate(
+            [
+                level[:frames] + below[:frames],
+                level[inner] + below[frames:] + above[: rows - 2 * frames],
+                level[rows - frames :] + above[rows - 2 * frames :],
+            ],
+            axis=0,
+        )
 
     def block_copy(m):
         return pltpu.make_async_remote_copy(
@@ -303,6 +306,8 @@
             await_edges(m, 1)
             finish(m, convolve(m, 1, 1, hmid[m], None))
 
+    for copy in small[:4]:
+        copy.wait()
     half = chans // 2
     slots = temb.shape[0]
     which = lax.broadcasted_iota(jnp.int32, (slots, half), 0)
@@ -315,7 +320,7 @@
         level = jnp.cos(math.pi / 2.0 * (steps_f / STEPS + 0.008) / 1.008) ** 2
         keep = jnp.sqrt(level)
         blur = jnp.sqrt(1.0 - level)
-        for copy in small[3:]:
+        for copy in small[4:]:
             copy.wait()
         for m in range(micros):
             noisy[m * rows_f : (m + 1) * rows_f, :] = (
@@ -332,16 +337,13 @@
 
     order = lax.broadcasted_iota(jnp.int32, (slots, half), 1).astype(jnp.float32)
     angles = steps_f * jnp.exp(-math.log(10000.0) * order / half)
-    for copy in small[:3]:
-        copy.wait()
     temb[...] = jnp.dot(
         jnp.sin(angles).astype(jnp.bfloat16), proj[0:half, :], preferred_element_type=jnp.float32
     ) + jnp.dot(
         jnp.cos(angles).astype(jnp.bfloat16), proj[half:chans, :], preferred_element_type=jnp.float32
     )
 
-    arrivals = n_time - 1
-    arrivals = arrivals + n_time * jnp.where(last, 0, 1) + n_time * jnp.where(first, 0, 1)
+    arrivals = n_time - 1 + n_time * jnp.where(last, 0, 1)
     pl.semaphore_wait(barrier, arrivals)
 
     @pl.when(first)
@@ -393,8 +395,8 @@
     dma = pltpu.SemaphoreType.DMA
     saved = pl.pallas_call(
         functools.partial(kernel, dims),
-        out_shape=jax.ShapeDtypeStruct((micros, rows, chans), jnp.bfloat16),
-        in_specs=[pl.BlockSpec(memory_space=pltpu.SMEM)] + [hbm] * 7,
+        out_shape=pltpu.VMEM((micros, rows, chans), jnp.bfloat16),
+        in_specs=[hbm] * 8,
         out_specs=vmem,
         scratch_shapes=[
             pltpu.VMEM((layers, 3, 3 * chans, chans), jnp.bfloat16),
@@ -408,7 +410,8 @@
             pltpu.VMEM((chans, chans), jnp.bfloat16),
             pltpu.VMEM((micros * rows_f, frames), jnp.float32),
             pltpu.VMEM((slots, chans), jnp.float32),
-            pltpu.VMEM((rows + 2 * frames, 3 * chans), jnp.bfloat16),
+            pltpu.SMEM((micros,), jnp.int32),
+            pltpu.VMEM((rows, 3 * chans), jnp.bfloat16),
             pltpu.VMEM((micros, 3, 1, 2 * chans), jnp.float32),
             pltpu.VMEM((micros, 2, n_time, 1, 2 * chans), jnp.float32),
             pltpu.VMEM((micros, 3, 2, rows_f, chans), jnp.float32),
@@ -420,20 +423,25 @@
             dma((micros,)),
             dma((micros,)),
             dma((layers,)),
-            dma((6,)),
+            dma((7,)),
         ],
         compiler_params=pltpu.CompilerParams(
-            collective_id=0, has_side_effects=True
+            collective_id=0, has_side_effects=True, vmem_limit_bytes=48 * 2**20
         ),
     )(
-        timestep,
-        clean,
-        noise,
-        lift.reshape(1, chans),
-        norm_gain,
-        norm_bias,
-        time_proj,
-        conv_weight.reshape(layers, 3, 3 * chans, chans),
+        *(
+            pltpu.with_memory_space_constraint(x, pltpu.HBM)
+            for x in (
+                timestep,
+                clean,
+                noise,
+                lift.reshape(1, chans),
+                norm_gain,
+                norm_bias,
+                time_proj,
+                conv_weight.reshape(layers, 3, 3 * chans, chans),
+            )
+        ),
     )
     return saved.reshape(1, micros, rows_f, frames, chans)
 

time: 46 us -> 42.9 us (0.933)
  Pallas kernels: 44 us -> 42 us
  local copies, waits for them, and re-layouts: 1.88 us -> 0.8 us
    pallas_call x1, Pallas kernels: 44 us -> 42 us  [on_device(): pl.pallas_call(functools.partial(kernel, dims), out_shape=pltpu.VMEM((mic...]
    unnamed x1, local copies, waits for them, and re-layouts: 1.88 us -> 0.8 us
where the time goes in v3:
time: 42.9 us; the launch traced here: 42.8 us
  Pallas kernels  42 us (98%)
  local copies, waits for them, and re-layouts  0.8 us (2%)
    pallas_call x1, Pallas kernels, on_device(): pl.pallas_call(functools.partial(kernel, dims), out_shape=pltpu.VMEM((mic...  42 us

profile of v3, /device:TPU:26, one launch (start us, length us, event | category | flops | bytes accessed | tf_op | source)
XLA Modules:
  0.0 42.8 jit_solution(10868403450727776165)
XLA Ops:
  0.0 42.0 %shard_map.82 = bf16[4,256,256]{2,1,0:T(8,128)(2,1)S(1)} custom-call(s32[4]{0:T(128)} %steps_in.1, f32[4,4,64]{2,1,0:T(4,128)} %clean_in.1, f32[4,4,64]{2,1,0:T(4,128)} %noise_in.1, f32[1,256]{1,0:T(1,128)} %bitcast.5, f32[1,2,256]{2,1,0:T(2,128)} %gains_in.1, f32[1,2,256]{2,1,0:T(2,128)} %biases_in.1, bf16[1,256,256]{2,1,0:T(8,128)(2,1)} %proj_in.1, ...), custom_call_target="tpu_custom_call" | custom-call | tf_op jit(solution)/shard_map/pallas_call | solution.py:396
  42.0 0.8 %copy.10 = bf16[1,4,4,64,256]{4,3,2,1,0:T(8,128)(2,1)} copy(bf16[1,4,4,64,256]{4,3,2,1,0:T(8,128)(2,1)S(1)} %bitcast.3) | data formatting | bytes 1048576

commit v4 on v3

--- a/solution.py
+++ b/solution.py
@@ -70,6 +70,7 @@
     up = jnp.minimum(sec + 1, n_section - 1)
     down = jnp.maximum(sec - 1, 0)
     short = n_time <= 8
+    pieces = 1
 
     def load_w(layer):
         return pltpu.make_async_copy(weights.at[layer], w.at[layer], w_sem.at[layer])
@@ -209,7 +210,7 @@
             step *= 2
         return total[0:1]
 
-    def convolve(m, slot, layer, hidden, shift_row):
+    def convolve(m, slot, layer, load, shift_row, parts):
         stats = jnp.sum(st_recv[m, slot], axis=0)
         s1 = stats[:, 0:chans]
         s2 = stats[:, chans : 2 * chans]
@@ -221,7 +222,6 @@
         var = total[:, chans : 2 * chans] / count - mean * mean
         scale = lax.rsqrt(var + 1e-05) * gains[layer : layer + 1, :]
         offset = biases[layer : layer + 1, :] - mean * scale
-        act = silu(hidden * scale + offset)
         edges = edge_recv[m, slot]
         if shift_row is not None:
             edges = edges + shift_row
@@ -229,37 +229,47 @@
         before = jnp.where(has_left, edges[0], 0.0)
         after = jnp.where(has_right, edges[1], 0.0)
         place = lax.broadcasted_iota(jnp.int32, (frames, chans), 0)
-        for f in range(rows_f):
-            part = act[f * frames : (f + 1) * frames]
-            prev = jnp.where(place == 0, before[f : f + 1], pltpu.roll(part, 1, 0))
-            nxt = jnp.where(place == frames - 1, after[f : f + 1], pltpu.roll(part, frames - 1, 0))
-            at = slice(f * frames, (f + 1) * frames)
-            act3[at, 0:chans] = prev.astype(jnp.bfloat16)
-            act3[at, chans : 2 * chans] = part.astype(jnp.bfloat16)
-            act3[at, 2 * chans : 3 * chans] = nxt.astype(jnp.bfloat16)
-        above, level, below = (
-            jnp.dot(act3[span], w[layer, i], preferred_element_type=jnp.float32)
-            for i, span in enumerate(
-                (slice(0, rows - frames), slice(0, rows), slice(frames, rows))
-            )
-        )
-        level = hidden + level
-        inner = slice(frames, rows - frames)
-        return jnp.concatenate(
-            [
-                level[:frames] + below[:frames],
-                level[inner] + below[frames:] + above[: rows - 2 * frames],
-                level[rows - frames :] + above[rows - 2 * frames :],
-            ],
-            axis=0,
-        )
-
-    def block_copy(m):
+        sums = [None] * rows_f
+
+        def add(f, value):
+            sums[f] = value if sums[f] is None else sums[f] + value
+
+        for part in range(parts):
+            low, high = part * rows_f // parts, (part + 1) * rows_f // parts
+            hidden = load(part, slice(low * frames, high * frames))
+            act = silu(hidden * scale + offset)
+            for f in range(low, high):
+                at = slice((f - low) * frames, (f - low + 1) * frames)
+                add(f, hidden[at])
+                row = act[at]
+                prev = jnp.where(place == 0, before[f : f + 1], pltpu.roll(row, 1, 0))
+                nxt = jnp.where(
+                    place == frames - 1, after[f : f + 1], pltpu.roll(row, frames - 1, 0)
+                )
+                at = slice(f * frames, (f + 1) * frames)
+                act3[at, 0:chans] = prev.astype(jnp.bfloat16)
+                act3[at, chans : 2 * chans] = row.astype(jnp.bfloat16)
+                act3[at, 2 * chans : 3 * chans] = nxt.astype(jnp.bfloat16)
+            for i in range(3):
+                used = [f for f in range(low, high) if 0 <= f - i + 1 < rows_f]
+                if not used:
+                    continue
+                span = slice(used[0] * frames, (used[-1] + 1) * frames)
+                product = jnp.dot(act3[span], w[layer, i], preferred_element_type=jnp.float32)
+                for k, f in enumerate(used):
+                    add(f - i + 1, product[k * frames : (k + 1) * frames])
+        return jnp.concatenate(sums, axis=0)
+
+    def piece(ref, m, part):
+        height = rows_f // pieces * frames
+        return ref.at[m, pl.ds(part * height, height)]
+
+    def block_copy(m, part):
         return pltpu.make_async_remote_copy(
-            src_ref=staged.at[m],
-            dst_ref=xin.at[m],
-            send_sem=blk_ssem.at[m],
-            recv_sem=blk_rsem.at[m],
+            src_ref=piece(staged, m, part),
+            dst_ref=piece(xin, m, part),
+            send_sem=blk_ssem.at[m, part],
+            recv_sem=blk_rsem.at[m, part],
             device_id=(up, tm),
             device_id_type=MESH,
         )
@@ -272,7 +282,8 @@
         def _():
             summarize(m, 2, rounded.astype(jnp.float32))
             publish(m, 2, 0, up, 0)
-            block_copy(m).start()
+            for part in range(pieces):
+                block_copy(m, part).start()
 
     def enter(m):
         @pl.when(first)
@@ -282,12 +293,19 @@
         @pl.when(jnp.logical_not(first))
         def _():
             await_stats(m, 0, 0)
-            pltpu.make_async_copy(xin.at[m], xin.at[m], blk_rsem.at[m]).wait()
 
         await_edges(m, 0)
         shift_row = temb[m : m + 1, :]
-        hidden = xin[m].astype(jnp.float32) + shift_row
-        hidden = convolve(m, 0, 0, hidden, shift_row)
+
+        def load(part, span):
+            @pl.when(jnp.logical_not(first))
+            def _():
+                landed = piece(xin, m, part)
+                pltpu.make_async_copy(landed, landed, blk_rsem.at[m, part]).wait()
+
+            return xin[m, span, :].astype(jnp.float32) + shift_row
+
+        hidden = convolve(m, 0, 0, load, shift_row, pieces)
 
         @pl.when(deep)
         def _():
@@ -304,7 +322,7 @@
         def _():
             await_stats(m, 1, 1)
             await_edges(m, 1)
-            finish(m, convolve(m, 1, 1, hmid[m], None))
+            finish(m, convolve(m, 1, 1, lambda part, span: hmid[m, span, :], None, 1))
 
     for copy in small[:4]:
         copy.wait()
@@ -378,7 +396,8 @@
     def _():
         for m in range(micros):
             drain(m, 2, 0)
-            block_copy(m).wait_send()
+            for part in range(pieces):
+                block_copy(m, part).wait_send()
 
 
 def on_device(clean, noise, timestep, lift, norm_gain, norm_bias, conv_weight, time_proj):
@@ -420,8 +439,8 @@
             dma((micros, 2)),
             dma((micros, 3, 2)),
             dma((micros, 2, 2)),
-            dma((micros,)),
-            dma((micros,)),
+            dma((micros, 2)),
+            dma((micros, 2)),
             dma((layers,)),
             dma((7,)),
         ],

time: 42.9 us -> 42.2 us (0.984)
  Pallas kernels: 42 us -> 41.2 us
    pallas_call x1, Pallas kernels: 42 us -> 41.2 us  [on_device(): pl.pallas_call(functools.partial(kernel, dims), out_shape=pltpu.VMEM((mic...]
where the time goes in v4:
time: 42.2 us; the launch traced here: 42 us
  Pallas kernels  41.2 us (98%)
  local copies, waits for them, and re-layouts  0.8 us (2%)
    pallas_call x1, Pallas kernels, on_device(): pl.pallas_call(functools.partial(kernel, dims), out_shape=pltpu.VMEM((mic...  41.2 us

profile of v4, /device:TPU:26, one launch (start us, length us, event | category | flops | bytes accessed | tf_op | source)
XLA Modules:
  0.0 42.0 jit_solution(16039078598105223915)
XLA Ops:
  0.0 41.2 %shard_map.82 = bf16[4,256,256]{2,1,0:T(8,128)(2,1)S(1)} custom-call(s32[4]{0:T(128)} %steps_in.1, f32[4,4,64]{2,1,0:T(4,128)} %clean_in.1, f32[4,4,64]{2,1,0:T(4,128)} %noise_in.1, f32[1,256]{1,0:T(1,128)} %bitcast.5, f32[1,2,256]{2,1,0:T(2,128)} %gains_in.1, f32[1,2,256]{2,1,0:T(2,128)} %biases_in.1, bf16[1,256,256]{2,1,0:T(8,128)(2,1)} %proj_in.1, ...), custom_call_target="tpu_custom_call" | custom-call | tf_op jit(solution)/shard_map/pallas_call | solution.py:415
  41.2 0.8 %copy.10 = bf16[1,4,4,64,256]{4,3,2,1,0:T(8,128)(2,1)} copy(bf16[1,4,4,64,256]{4,3,2,1,0:T(8,128)(2,1)S(1)} %bitcast.3) | data formatting | bytes 1048576
